TPU v7x, 32 devices: a whole 2x2x4 slice. The times are simulated.
32 devices in a mesh: sec: 4 (over x, core), key: 8 (over z, y).
Axes of the slice: x: 2, y: 2, z: 4, core: 2. Of those that a mesh axis runs over, the one named last changes fastest.
Arguments:
- query: bfloat16 [4096, 16, 128], P(('sec', 'key')), may hold values from -64 to 64
- key: bfloat16 [4096, 4, 128], P(('sec', 'key')), may hold values from -5 to 5
- value: bfloat16 [4096, 4, 128], P(('sec', 'key')), may hold values from -5 to 5
- raw_directions: bfloat16 [4096, 4, 128], P(('sec', 'key')), may hold values from -5 to 5
- beta_raw_logits: float32 [4096, 4], P(('sec', 'key')), may hold values from -7 to 7
Outputs:
- attended: bfloat16 [4096, 16, 128], P(('sec', 'key'))
All inputs are finite; a program needn't handle non-finite values.
Results may differ from a plain program's by a relative error of at most 0.0055.
Values sent between devices are 32-bit elements; how exact they have to be, the bound alone decides.
No kernel may reach another device: no remote copies, remote signals or barrier semaphores. Data moves between devices by JAX's collectives and lax.ppermute only.
A program may use at most 64 MiB of HBM per device.

v0:
```python
import math
import jax
import jax.numpy as jnp
from jax import lax
from jax.sharding import PartitionSpec as P

highest = lax.Precision.HIGHEST


def carried_in(value, axis, join, neutral, backward):
    count, mine = (lax.axis_size(axis), lax.axis_index(axis))
    pieces = lax.all_gather(value, axis)
    if backward:
        pieces = pieces[::-1]
        mine = count - 1 - mine
    total = jnp.full_like(value, 0) + jnp.asarray(neutral, value.dtype)

    def turn(position, total):
        longer = join(total, pieces[position])
        return jnp.where(position < mine, longer, total)

    return lax.fori_loop(0, count - 1, turn, total)


def shifted(value, axis, steps):
    count = lax.axis_size(axis)
    first, last = (max(0, -steps), min(count, count - steps))
    return lax.ppermute(value, axis, [(source, source + steps) for source in range(first, last)])


def block_terms(query, key, raw_directions, beta_raw_logits):
    length = key.shape[0]
    heads = key.shape[1]
    width = key.shape[2]
    query_group = query.shape[1] // heads
    w_float = raw_directions.astype(jnp.float32)
    w_unit = w_float / jnp.sqrt(jnp.sum(w_float * w_float, -1, keepdims=True) + 1e-06)
    beta = 2.0 * jax.nn.sigmoid(beta_raw_logits)
    w_heads = jnp.transpose(w_unit, (1, 0, 2))
    k_heads = jnp.transpose(key.astype(jnp.float32), (1, 0, 2))
    b_heads = jnp.transpose(beta, (1, 0))[:, :, None]
    positions = jnp.arange(length)
    strict = (positions[:, None] > positions[None, :]).astype(jnp.float32)
    lower = (positions[:, None] >= positions[None, :]).astype(jnp.float32)
    gram = jnp.einsum("hte,hse->hts", w_heads, w_heads, precision=highest) * strict
    system = jnp.eye(length, dtype=jnp.float32) + b_heads * gram
    cross = jnp.einsum("hte,hse->hts", w_heads, k_heads, precision=highest) * strict
    right = jnp.concatenate([b_heads * w_heads, b_heads * cross], axis=2)
    solved = lax.linalg.triangular_solve(
        system, right, left_side=True, lower=True, unit_diagonal=True
    )
    y_rows = solved[:, :, :width]
    z_rows = solved[:, :, width:]
    block_map = jnp.eye(width, dtype=jnp.float32) - jnp.einsum(
        "hte,htf->hef", w_heads, y_rows, precision=highest
    )
    key_end = k_heads - jnp.einsum("hts,hte->hse", z_rows, w_heads, precision=highest)
    q_heads = jnp.transpose(
        query.astype(jnp.float32).reshape(length, heads, query_group, width), (1, 2, 0, 3)
    )
    q_dot_w = jnp.einsum("hgie,hte->hgit", q_heads, w_heads, precision=highest) * lower
    query_start = q_heads - jnp.einsum("hgit,hte->hgie", q_dot_w, y_rows, precision=highest)
    inner = jnp.einsum("hgie,hje->hgij", q_heads, k_heads, precision=highest)
    inner = inner - jnp.einsum("hgit,htj->hgij", q_dot_w, z_rows, precision=highest)
    query_start = query_start.reshape(heads, query_group * length, width)
    inner = inner.reshape(heads, query_group * length, length) * width ** (-0.5)
    return (query_start, key_end, block_map, inner)


def attend(state, scores, values, valid):
    score_maxima, weighted_totals, exponent_sums = state
    masked = jnp.where(valid, scores, -1e30)
    new_max = jnp.maximum(score_maxima, jnp.max(masked, -1))
    weights = jnp.where(valid, jnp.exp(masked - new_max[..., None]), 0.0)
    factor = jnp.exp(score_maxima - new_max)
    weighted_totals = weighted_totals * factor + jnp.sum(weights, -1)
    rounded = weights.astype(jnp.bfloat16)
    exponent_sums = exponent_sums * factor[..., None] + jnp.einsum(
        "...ij,...je->...ie", rounded, values, preferred_element_type=jnp.float32
    )
    return (new_max, weighted_totals, exponent_sums)


def attend_packet(state, queries_flat, packet, valid, width):
    count = packet.shape[0]
    block = math.gcd(count, 512)
    scale_factor = width ** (-0.5)

    def one_block(index, carry):
        piece = lax.dynamic_slice_in_dim(packet, index * block, block, 0)
        scores = (
            jnp.einsum("ie,je->ij", queries_flat, piece[:, :width], precision=highest)
            * scale_factor
        )
        return attend(carry, scores, piece[:, width:].astype(jnp.bfloat16), valid)

    return lax.fori_loop(0, count // block, one_block, state)


def later_first(earlier, later):
    return jnp.einsum("hij,hjk->hik", later, earlier, precision=highest)


def earlier_first(earlier, later):
    return jnp.einsum("hij,hjk->hik", earlier, later, precision=highest)


def body(query, key, value, raw_directions, beta_raw_logits):
    length = query.shape[0]
    q_count = query.shape[1]
    width = query.shape[2]
    kv_heads = key.shape[1]
    query_group = q_count // kv_heads
    key_count = lax.axis_size("key")
    sec_count = lax.axis_size("sec")
    key_index = lax.axis_index("key")
    sec_index = lax.axis_index("sec")
    per_slot = q_count // key_count
    repeat_count = key_count // kv_heads
    rows_section = length * key_count
    scale_factor = width ** (-0.5)
    query_start, key_end, block_map, inner = block_terms(
        query, key, raw_directions, beta_raw_logits
    )
    value_head_rows = jnp.transpose(value, (1, 0, 2))
    positions = jnp.arange(length)
    causal = jnp.tile(positions[:, None] >= positions[None, :], (query_group, 1))
    local = (
        jnp.full((kv_heads, query_group * length), -1e30, jnp.float32),
        jnp.zeros((kv_heads, query_group * length), jnp.float32),
        jnp.zeros((kv_heads, query_group * length, width), jnp.float32),
    )
    local = attend(local, inner, value_head_rows, causal)
    packed = jnp.concatenate([key_end, value_head_rows.astype(jnp.float32)], axis=2)
    gathered_pack, gathered_maps = (
        lax.all_gather(packed, "key", axis=1, tiled=True),
        lax.all_gather(block_map, "key", axis=0, tiled=True),
    )
    gathered_maps = gathered_maps.reshape(key_count, kv_heads, width, width)

    def replay_step(step, carry):
        moving = carry[0]
        source = jnp.maximum(key_index - step, 0)
        piece = lax.dynamic_slice_in_dim(gathered_pack, source * length, length, 1)
        scores = (
            jnp.einsum("hie,hje->hij", moving, piece[:, :, :width], precision=highest)
            * scale_factor
        )
        state = attend(
            carry[1:], scores, piece[:, :, width:].astype(jnp.bfloat16), key_index - step >= 0
        )
        source_map = lax.dynamic_index_in_dim(gathered_maps, source, 0, keepdims=False)
        moving = jnp.einsum("hie,hef->hif", moving, source_map, precision=highest)
        return (moving,) + state

    local = lax.fori_loop(1, key_count, replay_step, (query_start,) + local)[1:]
    eye_maps = jnp.broadcast_to(jnp.eye(width, dtype=jnp.float32), block_map.shape)
    before = carried_in(block_map, "key", later_first, eye_maps, False)
    after = carried_in(block_map, "key", earlier_first, eye_maps, True)
    section_map = jnp.einsum(
        "hij,hjk->hik",
        after,
        jnp.einsum("hij,hjk->hik", block_map, before, precision=highest),
        precision=highest,
    )
    query_section = jnp.einsum("hie,hef->hif", query_start, before, precision=highest)
    query_section = jnp.transpose(
        query_section.reshape(kv_heads, query_group, length, width), (2, 0, 1, 3)
    )
    key_section = jnp.einsum("hje,hfe->hjf", key_end, after, precision=highest)
    key_pack = jnp.concatenate(
        [jnp.transpose(key_section, (1, 0, 2)), value.astype(jnp.float32)], axis=2
    )
    own_map = lax.dynamic_index_in_dim(section_map, key_index // repeat_count, 0, keepdims=False)
    query_slots = query_section.reshape(length, key_count, per_slot, width)
    key_slots = jnp.repeat(key_pack, repeat_count, axis=1)
    slot_queries, slot_keys = (
        lax.all_to_all(query_slots, "key", split_axis=1, concat_axis=0, tiled=True),
        lax.all_to_all(key_slots, "key", split_axis=1, concat_axis=0, tiled=True),
    )
    slot_flat = jnp.transpose(
        slot_queries.reshape(rows_section, per_slot, width), (1, 0, 2)
    ).reshape(per_slot * rows_section, width)
    slot_keys = slot_keys.reshape(rows_section, 2 * width)
    flat_rows = slot_flat.shape[0]
    distant = (
        jnp.full((flat_rows,), -1e30, jnp.float32),
        jnp.zeros((flat_rows,), jnp.float32),
        jnp.zeros((flat_rows, width), jnp.float32),
    )

    def walk_step(step, carry):
        arrived = shifted(carry[0], "sec", 1)
        state = attend_packet(carry[1:], slot_flat, arrived, sec_index - step >= 0, width)
        moved = jnp.einsum("je,fe->jf", arrived[:, :width], own_map, precision=highest)
        return (jnp.concatenate([moved, arrived[:, width:]], axis=1),) + state

    distant = lax.fori_loop(1, sec_count, walk_step, (slot_keys,) + distant)[1:]
    far_max = jnp.transpose(distant[0].reshape(per_slot, rows_section), (1, 0))
    far_total = jnp.transpose(distant[1].reshape(per_slot, rows_section), (1, 0))
    far_sums = jnp.transpose(distant[2].reshape(per_slot, rows_section, width), (1, 0, 2))
    back_sums, back_max, back_total = (
        lax.all_to_all(far_sums, "key", split_axis=0, concat_axis=1, tiled=True),
        lax.all_to_all(far_max, "key", split_axis=0, concat_axis=1, tiled=True),
        lax.all_to_all(far_total, "key", split_axis=0, concat_axis=1, tiled=True),
    )
    near_max = jnp.transpose(local[0].reshape(kv_heads, query_group, length), (2, 0, 1)).reshape(
        length, q_count
    )
    near_total = jnp.transpose(local[1].reshape(kv_heads, query_group, length), (2, 0, 1)).reshape(
        length, q_count
    )
    near_sums = jnp.transpose(
        local[2].reshape(kv_heads, query_group, length, width), (2, 0, 1, 3)
    ).reshape(length, q_count, width)
    joint_max = jnp.maximum(near_max, back_max)
    near_factor = jnp.exp(near_max - joint_max)
    far_factor = jnp.exp(back_max - joint_max)
    weighted_totals = near_total * near_factor + back_total * far_factor
    exponent_sums = near_sums * near_factor[..., None] + back_sums * far_factor[..., None]
    return (exponent_sums / weighted_totals[..., None]).astype(jnp.bfloat16)


def solution(mesh):
    return jax.shard_map(
        body,
        mesh=mesh,
        in_specs=(
            P(("sec", "key"), None, None),
            P(("sec", "key"), None, None),
            P(("sec", "key"), None, None),
            P(("sec", "key"), None, None),
            P(("sec", "key"), None),
        ),
        out_specs=P(("sec", "key"), None, None),
        check_vma=False,
    )
```

profile of v0, /device:TPU:6, one launch (start us, length us, event | category | flops | bytes accessed | tf_op | source)
XLA Modules:
  0.0 414.8 jit_solution(6768845351763684802)
XLA Ops:
  11.4 39.3 %custom-call.3 = f32[4,1,128,128]{2,3,1,0:T(8,128)S(1)} custom-call(f32[4,1,128,128]{3,2,1,0:T(8,128)S(1)} %fusion.41), custom_call_target="InvertDiagBlocksLowerTriangular" | custom-call | tf_op jit(solution)/shard_map/triangular_solve | solution.py:49
  60.5 44.1 %all-gather.4.cloned.1.call-done = f32[32,128,128]{2,1,0:T(8,128)} async-done(((f32[4,128,128]{2,1,0:T(8,128)}), f32[32,128,128]{2,1,0:T(8,128)}) %all-gather.4.cloned.1.call-update) | async-done | bytes 2097168 | tf_op jit(solution)/shard_map/all_gather | solution.py:137
  107.8 9.8 %while.97 = (s32[]{:T(128)}, f32[4,128,128]{2,1,0:T(8,128)S(1)}, s32[]{:T(128)}, f32[8,4,128,128]{3,2,1,0:T(8,128)}, s32[]{:T(128)}) while((s32[]{:T(128)}, f32[4,128,128]{2,1,0:T(8,128)S(1)}, s32[]{:T(128)}, f32[8,4,128,128]{3,2,1,0:T(8,128)}, s32[]{:T(128)}) %tuple.182), condition=%wide.region_10.11_spmd, body=%wide.region_9.10_spmd.sunk | while | flops 100728832 | bytes 1573447 | solution.py:22
  119.6 4.9 %all-to-all-start.1 = ((f32[128,8,2,128]{3,0,2,1:T(8,128)}), f32[128,8,2,128]{3,0,2,1:T(8,128)S(1)}, u32[]{:S(2)}, u32[]{:S(2)}) async-start(f32[128,8,2,128]{3,0,2,1:T(8,128)} %bitcast.46), calls=%async_computation.1 | async-start | bytes 2097152 | tf_op jit(solution)/shard_map/all_to_all | solution.py:178
  124.6 11.2 %while.96 = (s32[]{:T(128)}, f32[4,128,128]{1,2,0:T(8,128)S(1)}, s32[]{:T(128)}, f32[8,4,128,128]{3,2,1,0:T(8,128)}, s32[]{:T(128)}) while((s32[]{:T(128)}, f32[4,128,128]{1,2,0:T(8,128)S(1)}, s32[]{:T(128)}, f32[8,4,128,128]{3,2,1,0:T(8,128)}, s32[]{:T(128)}) %tuple.165), condition=%wide.region_8.9_spmd, body=%wide.region_7.8_spmd.sunk | while | flops 100728832 | bytes 1573447 | solution.py:22
  136.5 12.3 %all-to-all-done.1 = f32[128,8,2,128]{3,0,2,1:T(8,128)S(1)} async-done(((f32[128,8,2,128]{3,0,2,1:T(8,128)}), f32[128,8,2,128]{3,0,2,1:T(8,128)S(1)}, u32[]{:S(2)}, u32[]{:S(2)}) %all-to-all-start.1) | async-done | bytes 1048608 | tf_op jit(solution)/shard_map/all_to_all | solution.py:178
  149.9 4.3 %all-to-all-start = ((f32[128,8,256]{0,2,1:T(8,128)}), f32[128,8,256]{0,2,1:T(8,128)S(1)}, u32[]{:S(2)}, u32[]{:S(2)}) async-start(f32[128,8,256]{0,2,1:T(8,128)} %bitcast.228), calls=%async_computation | async-start | bytes 2097152 | tf_op jit(solution)/shard_map/all_to_all | solution.py:179
  157.3 36.5 %all-to-all-done = f32[128,8,256]{0,2,1:T(8,128)S(1)} async-done(((f32[128,8,256]{0,2,1:T(8,128)}), f32[128,8,256]{0,2,1:T(8,128)S(1)}, u32[]{:S(2)}, u32[]{:S(2)}) %all-to-all-start) | async-done | bytes 1048608 | tf_op jit(solution)/shard_map/all_to_all | solution.py:179
  195.5 122.5 %while.99 = (s32[]{:T(128)}, f32[1024,256]{0,1:T(8,128)S(1)}, f32[2048]{0:T(1024)S(1)}, f32[2048]{0:T(1024)S(1)}, f32[2048,128]{1,0:T(8,128)}, /*index=5*/f32[12...) while((s32[]{:T(128)}, f32[1024,256]{0,1:T(8,128)S(1)}, ...), condition=%wide.region_16.17_spmd, body=%wide.region_11.16_spmd.sunk | while | flops 2094796800 | bytes 44106204 | solution.py:198
  197.4 14.2 %collective-permute-done = f32[1024,256]{0,1:T(8,128)S(1)} collective-permute-done((f32[1024,256]{0,1:T(8,128)S(1)}, f32[1024,256]{0,1:T(8,128)S(1)}, u32[]{:S(2)}, u32[]{:S(2)}) %collective-permute-start) | collective-permute-done | bytes 1048608 | tf_op jit(solution)/shard_map/while/body/eval_jaxpr/ppermute | solution.py:28
  211.6 24.0 %while.100 = (s32[]{:T(128)}, f32[2048]{0:T(1024)S(1)}, f32[2048]{0:T(1024)S(1)}, f32[2048,128]{1,0:T(8,128)}, pred[]{:T(512)}, /*index=5*/f32[1024,256]{0,1:T(8...) while((s32[]{:T(128)}, f32[2048]{0:T(1024)S(1)}, ...), condition=%wide.region_15.15_spmd, body=%wide.region_12.14_spmd.sunk | while | flops 1893208064 | bytes 35651772 | solution.py:97
  218.8 4.9 %convolution_add_fusion.6 = f32[2048,128]{1,0:T(8,128)} fusion(f32[512,2048]{1,0:T(8,128)} %copy-done, f32[2048]{0:T(1024)S(1)} %max.48, pred[]{:T(512)} %get-tuple-element.1047, f32[2048,128]{1,0:T(8,128)} %get-tuple-element.1035, f32[2048]{0:T(1024)S(1)} %get-tuple-element.1020, bf16[512,128]{1,0:T(8,128)(2,1)S(1)} %copy.255), kind=kOutput, calls=%fused_computation.33.clone.1 | convolution fusion | flops 274202624 | bytes 6438913 | tf_op jit(solution)/shard_map/while/body/eval_jaxpr/while/body/eval_jaxpr/...ij,...je->...ie/dot_general | solution.py:78
  230.8 4.9 %convolution_add_fusion.6 = f32[2048,128]{1,0:T(8,128)} fusion(f32[512,2048]{1,0:T(8,128)} %copy-done, f32[2048]{0:T(1024)S(1)} %max.48, pred[]{:T(512)} %get-tuple-element.1047, f32[2048,128]{1,0:T(8,128)} %get-tuple-element.1035, f32[2048]{0:T(1024)S(1)} %get-tuple-element.1020, bf16[512,128]{1,0:T(8,128)(2,1)S(1)} %copy.255), kind=kOutput, calls=%fused_computation.33.clone.1 | convolution fusion | flops 274202624 | bytes 6438913 | tf_op jit(solution)/shard_map/while/body/eval_jaxpr/while/body/eval_jaxpr/...ij,...je->...ie/dot_general | solution.py:78
  238.3 14.2 %collective-permute-done = f32[1024,256]{0,1:T(8,128)S(1)} collective-permute-done((f32[1024,256]{0,1:T(8,128)S(1)}, f32[1024,256]{0,1:T(8,128)S(1)}, u32[]{:S(2)}, u32[]{:S(2)}) %collective-permute-start) | collective-permute-done | bytes 1048608 | tf_op jit(solution)/shard_map/while/body/eval_jaxpr/ppermute | solution.py:28
  252.5 24.0 %while.100 = (s32[]{:T(128)}, f32[2048]{0:T(1024)S(1)}, f32[2048]{0:T(1024)S(1)}, f32[2048,128]{1,0:T(8,128)}, pred[]{:T(512)}, /*index=5*/f32[1024,256]{0,1:T(8...) while((s32[]{:T(128)}, f32[2048]{0:T(1024)S(1)}, ...), condition=%wide.region_15.15_spmd, body=%wide.region_12.14_spmd.sunk | while | flops 1893208064 | bytes 35651772 | solution.py:97
  259.7 4.8 %convolution_add_fusion.6 = f32[2048,128]{1,0:T(8,128)} fusion(f32[512,2048]{1,0:T(8,128)} %copy-done, f32[2048]{0:T(1024)S(1)} %max.48, pred[]{:T(512)} %get-tuple-element.1047, f32[2048,128]{1,0:T(8,128)} %get-tuple-element.1035, f32[2048]{0:T(1024)S(1)} %get-tuple-element.1020, bf16[512,128]{1,0:T(8,128)(2,1)S(1)} %copy.255), kind=kOutput, calls=%fused_computation.33.clone.1 | convolution fusion | flops 274202624 | bytes 6438913 | tf_op jit(solution)/shard_map/while/body/eval_jaxpr/while/body/eval_jaxpr/...ij,...je->...ie/dot_general | solution.py:78
  271.6 4.8 %convolution_add_fusion.6 = f32[2048,128]{1,0:T(8,128)} fusion(f32[512,2048]{1,0:T(8,128)} %copy-done, f32[2048]{0:T(1024)S(1)} %max.48, pred[]{:T(512)} %get-tuple-element.1047, f32[2048,128]{1,0:T(8,128)} %get-tuple-element.1035, f32[2048]{0:T(1024)S(1)} %get-tuple-element.1020, bf16[512,128]{1,0:T(8,128)(2,1)S(1)} %copy.255), kind=kOutput, calls=%fused_computation.33.clone.1 | convolution fusion | flops 274202624 | bytes 6438913 | tf_op jit(solution)/shard_map/while/body/eval_jaxpr/while/body/eval_jaxpr/...ij,...je->...ie/dot_general | solution.py:78
  279.2 14.2 %collective-permute-done = f32[1024,256]{0,1:T(8,128)S(1)} collective-permute-done((f32[1024,256]{0,1:T(8,128)S(1)}, f32[1024,256]{0,1:T(8,128)S(1)}, u32[]{:S(2)}, u32[]{:S(2)}) %collective-permute-start) | collective-permute-done | bytes 1048608 | tf_op jit(solution)/shard_map/while/body/eval_jaxpr/ppermute | solution.py:28
  293.3 24.0 %while.100 = (s32[]{:T(128)}, f32[2048]{0:T(1024)S(1)}, f32[2048]{0:T(1024)S(1)}, f32[2048,128]{1,0:T(8,128)}, pred[]{:T(512)}, /*index=5*/f32[1024,256]{0,1:T(8...) while((s32[]{:T(128)}, f32[2048]{0:T(1024)S(1)}, ...), condition=%wide.region_15.15_spmd, body=%wide.region_12.14_spmd.sunk | while | flops 1893208064 | bytes 35651772 | solution.py:97
  300.5 4.8 %convolution_add_fusion.6 = f32[2048,128]{1,0:T(8,128)} fusion(f32[512,2048]{1,0:T(8,128)} %copy-done, f32[2048]{0:T(1024)S(1)} %max.48, pred[]{:T(512)} %get-tuple-element.1047, f32[2048,128]{1,0:T(8,128)} %get-tuple-element.1035, f32[2048]{0:T(1024)S(1)} %get-tuple-element.1020, bf16[512,128]{1,0:T(8,128)(2,1)S(1)} %copy.255), kind=kOutput, calls=%fused_computation.33.clone.1 | convolution fusion | flops 274202624 | bytes 6438913 | tf_op jit(solution)/shard_map/while/body/eval_jaxpr/while/body/eval_jaxpr/...ij,...je->...ie/dot_general | solution.py:78
  312.5 4.8 %convolution_add_fusion.6 = f32[2048,128]{1,0:T(8,128)} fusion(f32[512,2048]{1,0:T(8,128)} %copy-done, f32[2048]{0:T(1024)S(1)} %max.48, pred[]{:T(512)} %get-tuple-element.1047, f32[2048,128]{1,0:T(8,128)} %get-tuple-element.1035, f32[2048]{0:T(1024)S(1)} %get-tuple-element.1020, bf16[512,128]{1,0:T(8,128)(2,1)S(1)} %copy.255), kind=kOutput, calls=%fused_computation.33.clone.1 | convolution fusion | flops 274202624 | bytes 6438913 | tf_op jit(solution)/shard_map/while/body/eval_jaxpr/while/body/eval_jaxpr/...ij,...je->...ie/dot_general | solution.py:78
  327.6 5.6 %all-to-all-start.3 = ((f32[1024,2,128]{2,1,0:T(2,128)}), f32[1024,2,128]{2,1,0:T(2,128)}, u32[]{:S(2)}, u32[]{:S(2)}) async-start(f32[1024,2,128]{2,1,0:T(2,128)} %copy.176), calls=%async_computation.3 | async-start | bytes 2097152 | tf_op jit(solution)/shard_map/all_to_all | solution.py:203
  337.8 11.0 %all-to-all-done.3 = f32[1024,2,128]{2,1,0:T(2,128)} async-done(((f32[1024,2,128]{2,1,0:T(2,128)}), f32[1024,2,128]{2,1,0:T(2,128)}, u32[]{:S(2)}, u32[]{:S(2)}) %all-to-all-start.3) | async-done | bytes 1048608 | tf_op jit(solution)/shard_map/all_to_all | solution.py:203
  353.0 51.2 %while.95 = (s32[]{:T(128)}, f32[4,512,128]{1,2,0:T(8,128)S(1)}, f32[4,512]{1,0:T(4,128)S(1)}, f32[4,512]{1,0:T(4,128)S(1)}, f32[4,512,128]{2,1,0:T(8,128)S(1)},...) while((s32[]{:T(128)}, f32[4,512,128]{1,2,0:T(8,128)S(1)}, ...), condition=%wide.region_6.7_spmd, body=%wide.region_3.6_spmd.sunk | while | flops 875302912 | bytes 15991019 | solution.py:156
  (314 shorter events, 169.4 us)
Async XLA Ops:
  6.5 47.1 %copy-start.9 = (bf16[128,4,128]{2,1,0:T(4,128)(2,1)S(1)}, bf16[128,4,128]{2,1,0:T(4,128)(2,1)}, u32[]{:S(2)}) copy-start(bf16[128,4,128]{2,1,0:T(4,128)(2,1)} %param.18) | copy-start | bytes 393220
  6.5 48.6 %copy-start.14 = (bf16[128,16,128]{2,1,0:T(8,128)(2,1)S(1)}, bf16[128,16,128]{2,1,0:T(8,128)(2,1)}, u32[]{:S(2)}) copy-start(bf16[128,16,128]{2,1,0:T(8,128)(2,1)} %param.15) | copy-start | bytes 1572868
  6.5 48.8 %copy-start.16 = (bf16[128,4,128]{2,1,0:T(4,128)(2,1)S(1)}, bf16[128,4,128]{2,1,0:T(4,128)(2,1)}, u32[]{:S(2)}) copy-start(bf16[128,4,128]{2,1,0:T(4,128)(2,1)} %param.17) | copy-start | bytes 393220
  6.5 98.0 %all-gather.4.cloned.1.call-start = ((), (), s32[]{:S(2)}) async-start(), calls=%async_computation.5 | async-start | bytes 2359296 | tf_op jit(solution)/shard_map/all_gather | solution.py:137
  53.6 6.8 %copy-start.7 = (f32[4,128,256]{2,1,0:T(8,128)}, f32[4,128,256]{2,1,0:T(8,128)S(1)}, u32[]{:S(2)}) copy-start(f32[4,128,256]{2,1,0:T(8,128)S(1)} %fusion.49) | copy-start | bytes 1572868
  55.3 52.4 %copy-start.5 = (bf16[128,16,128]{2,0,1:T(8,128)(2,1)}, bf16[128,16,128]{2,0,1:T(8,128)(2,1)S(1)}, u32[]{:S(2)}) copy-start(bf16[128,16,128]{2,0,1:T(8,128)(2,1)S(1)} %copy.148) | copy-start | bytes 1572868
  55.5 49.1 %copy-start.10 = (bf16[128,4,128]{0,2,1:T(8,128)(2,1)}, bf16[128,4,128]{0,2,1:T(8,128)(2,1)S(1)}, u32[]{:S(2)}) copy-start(bf16[128,4,128]{0,2,1:T(8,128)(2,1)S(1)} %copy.204) | copy-start | bytes 393220
  57.0 78.9 %copy-start.13 = (f32[4,128,128]{1,2,0:T(8,128)}, f32[4,128,128]{1,2,0:T(8,128)S(1)}, u32[]{:S(2)}) copy-start(f32[4,128,128]{1,2,0:T(8,128)S(1)} %convolution_subtract_fusion.2) | copy-start | bytes 786436
  60.4 57.2 %copy-start.4 = (f32[4,4,128,128]{3,2,1,0:T(8,128)}, f32[4,4,128,128]{3,2,1,0:T(8,128)S(1)}, u32[]{:S(2)}) copy-start(f32[4,4,128,128]{3,2,1,0:T(8,128)S(1)} %convolution_subtract_fusion.1) | copy-start | bytes 3145732
  119.6 29.2 %all-to-all-start.1 = ((f32[128,8,2,128]{3,0,2,1:T(8,128)}), f32[128,8,2,128]{3,0,2,1:T(8,128)S(1)}, u32[]{:S(2)}, u32[]{:S(2)}) async-start(f32[128,8,2,128]{3,0,2,1:T(8,128)} %bitcast.46), calls=%async_computation.1 | async-start | bytes 2097152 | tf_op jit(solution)/shard_map/all_to_all | solution.py:178
  135.8 20.3 %copy-start.12 = (f32[4,128,128]{2,1,0:T(8,128)S(1)}, f32[4,128,128]{2,1,0:T(8,128)}, u32[]{:S(2)}) copy-start(f32[4,128,128]{2,1,0:T(8,128)} %convolution_subtract_fusion.3) | copy-start | bytes 786436
  149.9 43.8 %all-to-all-start = ((f32[128,8,256]{0,2,1:T(8,128)}), f32[128,8,256]{0,2,1:T(8,128)S(1)}, u32[]{:S(2)}, u32[]{:S(2)}) async-start(f32[128,8,256]{0,2,1:T(8,128)} %bitcast.228), calls=%async_computation | async-start | bytes 2097152 | tf_op jit(solution)/shard_map/all_to_all | solution.py:179
  154.2 198.8 %all-gather.6.cloned.1.call-start = ((), (), s32[]{:S(2)}) async-start(), calls=%async_computation.6 | async-start | bytes 4718592 | tf_op jit(solution)/shard_map/all_gather | solution.py:136
  195.5 16.1 %collective-permute-start = (f32[1024,256]{0,1:T(8,128)S(1)}, f32[1024,256]{0,1:T(8,128)S(1)}, u32[]{:S(2)}, u32[]{:S(2)}) collective-permute-start(f32[1024,256]{0,1:T(8,128)S(1)} %get-tuple-element.1099), channel_id=1, source_target_pairs={{0,8},{8,16},{16,24},{1,9},{9,17},{17,25},{2,10},{10,18},{18,26},{... | collective-permute-start | bytes 3145736 | tf_op jit(solution)/shard_map/while/body/eval_jaxpr/ppermute | solution.py:28
  236.4 16.1 %collective-permute-start = (f32[1024,256]{0,1:T(8,128)S(1)}, f32[1024,256]{0,1:T(8,128)S(1)}, u32[]{:S(2)}, u32[]{:S(2)}) collective-permute-start(f32[1024,256]{0,1:T(8,128)S(1)} %get-tuple-element.1099), channel_id=1, source_target_pairs={{0,8},{8,16},{16,24},{1,9},{9,17},{17,25},{2,10},{10,18},{18,26},{... | collective-permute-start | bytes 3145736 | tf_op jit(solution)/shard_map/while/body/eval_jaxpr/ppermute | solution.py:28
  277.2 16.1 %collective-permute-start = (f32[1024,256]{0,1:T(8,128)S(1)}, f32[1024,256]{0,1:T(8,128)S(1)}, u32[]{:S(2)}, u32[]{:S(2)}) collective-permute-start(f32[1024,256]{0,1:T(8,128)S(1)} %get-tuple-element.1099), channel_id=1, source_target_pairs={{0,8},{8,16},{16,24},{1,9},{9,17},{17,25},{2,10},{10,18},{18,26},{... | collective-permute-start | bytes 3145736 | tf_op jit(solution)/shard_map/while/body/eval_jaxpr/ppermute | solution.py:28
  318.0 15.4 %copy-start.3 = (f32[4,4,128,128]{2,3,1,0:T(8,128)S(1)}, f32[4,4,128,128]{2,3,1,0:T(8,128)}, u32[]{:S(2)}) copy-start(f32[4,4,128,128]{2,3,1,0:T(8,128)} %copy-done.2) | copy-start | bytes 3145732
  318.0 15.4 %copy-start.8 = (f32[4,128,256]{2,1,0:T(8,128)S(1)}, f32[4,128,256]{2,1,0:T(8,128)}, u32[]{:S(2)}) copy-start(f32[4,128,256]{2,1,0:T(8,128)} %copy-done.7) | copy-start | bytes 1572868
  318.7 9.0 %all-to-all-start.2 = ((f32[8,128,2]{1,2,0:T(2,128)}), f32[8,128,2]{1,2,0:T(2,128)S(1)}, u32[]{:S(2)}, u32[]{:S(2)}) async-start(f32[8,128,2]{1,2,0:T(2,128)} %bitcast.53), calls=%async_computation.2 | async-start | bytes 16384 | tf_op jit(solution)/shard_map/all_to_all | solution.py:204
  322.5 12.7 %copy-start.6 = (bf16[128,16,128]{2,0,1:T(8,128)(2,1)S(1)}, bf16[128,16,128]{2,0,1:T(8,128)(2,1)}, u32[]{:S(2)}) copy-start(bf16[128,16,128]{2,0,1:T(8,128)(2,1)} %copy-done.5) | copy-start | bytes 1572868
  322.5 12.7 %copy-start.15 = (bf16[128,4,128]{2,1,0:T(4,128)(2,1)S(1)}, bf16[128,4,128]{2,1,0:T(4,128)(2,1)}, u32[]{:S(2)}) copy-start(bf16[128,4,128]{2,1,0:T(4,128)(2,1)} %param.16) | copy-start | bytes 393220
  327.6 21.2 %all-to-all-start.3 = ((f32[1024,2,128]{2,1,0:T(2,128)}), f32[1024,2,128]{2,1,0:T(2,128)}, u32[]{:S(2)}, u32[]{:S(2)}) async-start(f32[1024,2,128]{2,1,0:T(2,128)} %copy.176), calls=%async_computation.3 | async-start | bytes 2097152 | tf_op jit(solution)/shard_map/all_to_all | solution.py:203
  333.2 3.6 copy-start.11
  348.8 56.9 %all-to-all-start.4 = ((f32[8,128,2]{1,2,0:T(2,128)}), f32[8,128,2]{1,2,0:T(2,128)S(1)}, u32[]{:S(2)}, u32[]{:S(2)}) async-start(f32[8,128,2]{1,2,0:T(2,128)} %bitcast.65), calls=%async_computation.4 | async-start | bytes 16384 | tf_op jit(solution)/shard_map/all_to_all | solution.py:205
  (14 other events, 18.7 us)
Sparse Core Ops, SparseCore 0:
  55.2 49.3 all-gather.3
  157.0 84.8 all-gather.5
where the time goes:
time: 417 us; the launch traced here: 415 us
  waiting for transfers between devices  147 us (35%)
  matrix products  115 us (28%)
  other arithmetic  54.8 us (13%)
  local copies, waits for them, and re-layouts  53.7 us (13%)
  starting transfers between devices  28.6 us (7%)
  between operations  13.9 us (3%)
    all_gather x1, waiting for transfers between devices, body(): lax.all_gather(block_map, 'key', axis=0, tiled=True)  44.1 us
    ppermute x3, waiting for transfers between devices, shifted(): lax.ppermute(value, axis, [(source, source + steps) for source in range(f...  42.5 us
    another operation x3, other arithmetic, block_terms(): lax.linalg.triangular_solve(system, right, left_side=True, lower=True, un...  39.4 us
    all_to_all x1, waiting for transfers between devices, body(): lax.all_to_all(key_slots, 'key', split_axis=1, concat_axis=0, tiled=True)  36.5 us
    dot_general x14, matrix products, attend(): jnp.einsum('...ij,...je->...ie', rounded, values, preferred_element_type=...  34.2 us
    dot_general x6, matrix products, one_block(): jnp.einsum('ie,je->ij', queries_flat, piece[:, :width], precision=highest)  22.7 us
    while x86, local copies, waits for them, and re-layouts  21.6 us
    dot_general x7, matrix products, replay_step(): moving = jnp.einsum('hie,hef->hif', moving, source_map, precision=highest)  14.3 us
  transfers between devices with their start and end apart: 10, of which 8 were waited for; matrix products, arithmetic and copies ran while one was open for 33% of the time, Pallas kernels for 0%

commit v1 on v0

--- a/solution.py
+++ b/solution.py
@@ -1,3 +1,4 @@
+import functools
 import math
 import jax
 import jax.numpy as jnp
@@ -5,6 +6,36 @@
 from jax.sharding import PartitionSpec as P
 
 highest = lax.Precision.HIGHEST
+
+
+def cover_plane_over_axis(array_in, mesh_ax):
+    rack = []
+    current_arr, side_arr, o_now = (
+        jax.lax.axis_size(mesh_ax),
+        jax.lax.axis_index(mesh_ax),
+        array_in.shape[0],
+    )
+    for i, p in enumerate(array_in.shape):
+        rack.append(p * current_arr if i == 0 else p)
+    idx = 1
+    u_next = lax.dynamic_update_slice_in_dim(
+        jnp.zeros(rack, array_in.dtype), array_in, side_arr * o_now, axis=0
+    )
+    while idx < current_arr:
+        line_up = []
+        i = 0
+        while i < current_arr:
+            line_up.append((i, (i + 1) % current_arr))
+            i = i + 1
+        array_in = jax.lax.ppermute(array_in, mesh_ax, line_up)
+        u_next = lax.dynamic_update_slice_in_dim(
+            u_next, array_in, (side_arr - idx) % current_arr * o_now, axis=0
+        )
+        idx += 1
+    return u_next
+
+
+tails_register = functools.partial(cover_plane_over_axis, mesh_ax="key")
 
 
 def carried_in(value, axis, join, neutral, backward):
@@ -134,7 +165,7 @@
     packed = jnp.concatenate([key_end, value_head_rows.astype(jnp.float32)], axis=2)
     gathered_pack, gathered_maps = (
         lax.all_gather(packed, "key", axis=1, tiled=True),
-        lax.all_gather(block_map, "key", axis=0, tiled=True),
+        tails_register(block_map),
     )
     gathered_maps = gathered_maps.reshape(key_count, kv_heads, width, width)
 

time: 417 us -> 469 us (1.12)
  waiting for transfers between devices: 147 us -> 171 us
  starting transfers between devices: 28.6 us -> 46.8 us
  local copies, waits for them, and re-layouts: 53.7 us -> 59.2 us
    ppermute x0 -> x7, waiting for transfers between devices: none -> 57.1 us  [cover_plane_over_axis(): array_in = jax.lax.ppermute(array_in, mesh_ax, line_up)]
    all_to_all x1, waiting for transfers between devices: 36.5 us -> 15.3 us  [body(): lax.all_to_all(key_slots, 'key', split_axis=1, concat_axis=0, tiled=True)]
    ppermute x0 -> x7, starting transfers between devices: none -> 14 us  [cover_plane_over_axis(): array_in = jax.lax.ppermute(array_in, mesh_ax, line_up)]
    all_to_all x1, waiting for transfers between devices: 11 us -> 0.01 us  [body(): lax.all_to_all(far_sums, 'key', split_axis=0, concat_axis=1, tiled=True)]
    while x86, local copies, waits for them, and re-layouts: 21.6 us -> 15.8 us
    dynamic_update_slice x0 -> x8, local copies, waits for them, and re-layouts: none -> 5.78 us  [the longest x7 5.06 us: cover_plane_over_axis(): lax.dynamic_update_slice_in_dim(u_next, array_in, (side_arr - idx) % curr...]
  transfers between devices with their start and end apart: 10 -> 17, of which waited for: 8 -> 13; matrix products, arithmetic and copies ran while one was open for 33% -> 33% of each run, Pallas kernels for 0% -> 0%
where the time goes in v1:
time: 469 us; the launch traced here: 466 us
  waiting for transfers between devices  171 us (36%)
  matrix products  116 us (25%)
  local copies, waits for them, and re-layouts  59.2 us (13%)
  other arithmetic  57.2 us (12%)
  starting transfers between devices  46.8 us (10%)
  between operations  14 us (3%)
    ppermute x7, waiting for transfers between devices, cover_plane_over_axis(): array_in = jax.lax.ppermute(array_in, mesh_ax, line_up)  57.1 us
    all_gather x1, waiting for transfers between devices, carried_in(): pieces = lax.all_gather(value, axis)  44.4 us
    ppermute x3, waiting for transfers between devices, shifted(): lax.ppermute(value, axis, [(source, source + steps) for source in range(f...  42.5 us
    another operation x3, other arithmetic, block_terms(): lax.linalg.triangular_solve(system, right, left_side=True, lower=True, un...  39.4 us
    dot_general x14, matrix products, attend(): jnp.einsum('...ij,...je->...ie', rounded, values, preferred_element_type=...  33.9 us
    dot_general x6, matrix products, one_block(): jnp.einsum('ie,je->ij', queries_flat, piece[:, :width], precision=highest)  22.7 us
    while x86, local copies, waits for them, and re-layouts  15.8 us
    all_to_all x1, waiting for transfers between devices, body(): lax.all_to_all(key_slots, 'key', split_axis=1, concat_axis=0, tiled=True)  15.3 us
  transfers between devices with their start and end apart: 17, of which 13 were waited for; matrix products, arithmetic and copies ran while one was open for 33% of the time, Pallas kernels for 0%

profile of v1, /device:TPU:6, one launch (start us, length us, event | category | flops | bytes accessed | tf_op | source)
XLA Modules:
  0.0 466.5 jit_solution(3632365724478160566)
XLA Ops:
  11.3 39.3 %custom-call.3 = f32[4,1,128,128]{2,3,1,0:T(8,128)S(1)} custom-call(f32[4,1,128,128]{3,2,1,0:T(8,128)S(1)} %fusion.41), custom_call_target="InvertDiagBlocksLowerTriangular" | custom-call | tf_op jit(solution)/shard_map/triangular_solve | solution.py:80
  58.4 44.4 %all-gather.6.cloned.1.call-done = f32[32,128,128]{2,1,0:T(8,128)} async-done(((f32[4,128,128]{2,1,0:T(8,128)}), f32[32,128,128]{2,1,0:T(8,128)}) %all-gather.6.cloned.1.call-update) | async-done | bytes 2097168 | tf_op jit(solution)/shard_map/all_gather | solution.py:43
  105.9 9.8 %while.97 = (s32[]{:T(128)}, f32[4,128,128]{2,1,0:T(8,128)S(1)}, s32[]{:T(128)}, f32[8,4,128,128]{3,2,1,0:T(8,128)}, s32[]{:T(128)}) while((s32[]{:T(128)}, f32[4,128,128]{2,1,0:T(8,128)S(1)}, s32[]{:T(128)}, f32[8,4,128,128]{3,2,1,0:T(8,128)}, s32[]{:T(128)}) %tuple.182), condition=%wide.region_10.11_spmd, body=%wide.region_9.10_spmd.sunk | while | flops 100728832 | bytes 1573447 | solution.py:53
  117.8 4.9 %all-to-all-start.1 = ((f32[128,8,2,128]{3,0,2,1:T(8,128)}), f32[128,8,2,128]{3,0,2,1:T(8,128)S(1)}, u32[]{:S(2)}, u32[]{:S(2)}) async-start(f32[128,8,2,128]{3,0,2,1:T(8,128)} %bitcast.229), calls=%async_computation.1 | async-start | bytes 2097152 | tf_op jit(solution)/shard_map/all_to_all | solution.py:209
  122.8 11.4 %while.96 = (s32[]{:T(128)}, f32[4,128,128]{1,2,0:T(8,128)S(1)}, s32[]{:T(128)}, f32[8,4,128,128]{3,2,1,0:T(8,128)}, s32[]{:T(128)}) while((s32[]{:T(128)}, f32[4,128,128]{1,2,0:T(8,128)S(1)}, s32[]{:T(128)}, f32[8,4,128,128]{3,2,1,0:T(8,128)}, s32[]{:T(128)}) %tuple.165), condition=%wide.region_8.9_spmd, body=%wide.region_7.8_spmd.sunk | while | flops 100728832 | bytes 1573447 | solution.py:53
  136.5 10.5 %all-to-all-done.1 = f32[128,8,2,128]{3,0,2,1:T(8,128)S(1)} async-done(((f32[128,8,2,128]{3,0,2,1:T(8,128)}), f32[128,8,2,128]{3,0,2,1:T(8,128)S(1)}, u32[]{:S(2)}, u32[]{:S(2)}) %all-to-all-start.1) | async-done | bytes 1048608 | tf_op jit(solution)/shard_map/all_to_all | solution.py:209
  149.1 4.9 %all-to-all-start = ((f32[128,8,256]{0,2,1:T(8,128)}), f32[128,8,256]{0,2,1:T(8,128)}, u32[]{:S(2)}, u32[]{:S(2)}) async-start(f32[128,8,256]{0,2,1:T(8,128)} %bitcast.228), calls=%async_computation | async-start | bytes 2097152 | tf_op jit(solution)/shard_map/all_to_all | solution.py:210
  163.9 20.5 %collective-permute-done.1 = f32[4,128,128]{2,1,0:T(8,128)} collective-permute-done((f32[4,128,128]{2,1,0:T(8,128)S(1)}, f32[4,128,128]{2,1,0:T(8,128)}, u32[]{:S(2)}, u32[]{:S(2)}) %collective-permute-start.1) | collective-permute-done | bytes 262176 | tf_op jit(solution)/shard_map/ppermute | solution.py:30
  188.9 15.3 %all-to-all-done = f32[128,8,256]{0,2,1:T(8,128)} async-done(((f32[128,8,256]{0,2,1:T(8,128)}), f32[128,8,256]{0,2,1:T(8,128)}, u32[]{:S(2)}, u32[]{:S(2)}) %all-to-all-start) | async-done | bytes 1048608 | tf_op jit(solution)/shard_map/all_to_all | solution.py:210
  207.2 116.6 %while.99 = (s32[]{:T(128)}, f32[1024,256]{0,1:T(8,128)S(1)}, f32[2048]{0:T(1024)S(1)}, f32[2048]{0:T(1024)S(1)}, f32[2048,128]{1,0:T(8,128)}, /*index=5*/f32[12...) while((s32[]{:T(128)}, f32[1024,256]{0,1:T(8,128)S(1)}, ...), condition=%wide.region_16.17_spmd, body=%wide.region_11.16_spmd.sunk | while | flops 2094796800 | bytes 44106204 | solution.py:229
  209.3 14.2 %collective-permute-done = f32[1024,256]{0,1:T(8,128)S(1)} collective-permute-done((f32[1024,256]{0,1:T(8,128)S(1)}, f32[1024,256]{0,1:T(8,128)S(1)}, u32[]{:S(2)}, u32[]{:S(2)}) %collective-permute-start) | collective-permute-done | bytes 1048608 | tf_op jit(solution)/shard_map/while/body/eval_jaxpr/ppermute | solution.py:59
  223.5 22.0 %while.100 = (s32[]{:T(128)}, f32[2048]{0:T(1024)S(1)}, f32[2048]{0:T(1024)S(1)}, f32[2048,128]{1,0:T(8,128)}, pred[]{:T(512)}, /*index=5*/f32[1024,256]{0,1:T(8...) while((s32[]{:T(128)}, f32[2048]{0:T(1024)S(1)}, ...), condition=%wide.region_15.15_spmd, body=%wide.region_12.14_spmd.sunk | while | flops 1893208064 | bytes 35651772 | solution.py:128
  240.6 4.8 %convolution_add_fusion.6 = f32[2048,128]{1,0:T(8,128)} fusion(f32[512,2048]{1,0:T(8,128)} %copy-done, f32[2048]{0:T(1024)S(1)} %max.48, pred[]{:T(512)} %get-tuple-element.1047, f32[2048,128]{1,0:T(8,128)} %get-tuple-element.1035, f32[2048]{0:T(1024)S(1)} %get-tuple-element.1020, bf16[512,128]{1,0:T(8,128)(2,1)S(1)} %copy.289), kind=kOutput, calls=%fused_computation.33.clone.1 | convolution fusion | flops 274202624 | bytes 6438913 | tf_op jit(solution)/shard_map/while/body/eval_jaxpr/while/body/eval_jaxpr/...ij,...je->...ie/dot_general | solution.py:109
  248.2 14.2 %collective-permute-done = f32[1024,256]{0,1:T(8,128)S(1)} collective-permute-done((f32[1024,256]{0,1:T(8,128)S(1)}, f32[1024,256]{0,1:T(8,128)S(1)}, u32[]{:S(2)}, u32[]{:S(2)}) %collective-permute-start) | collective-permute-done | bytes 1048608 | tf_op jit(solution)/shard_map/while/body/eval_jaxpr/ppermute | solution.py:59
  262.3 21.9 %while.100 = (s32[]{:T(128)}, f32[2048]{0:T(1024)S(1)}, f32[2048]{0:T(1024)S(1)}, f32[2048,128]{1,0:T(8,128)}, pred[]{:T(512)}, /*index=5*/f32[1024,256]{0,1:T(8...) while((s32[]{:T(128)}, f32[2048]{0:T(1024)S(1)}, ...), condition=%wide.region_15.15_spmd, body=%wide.region_12.14_spmd.sunk | while | flops 1893208064 | bytes 35651772 | solution.py:128
  286.9 14.2 %collective-permute-done = f32[1024,256]{0,1:T(8,128)S(1)} collective-permute-done((f32[1024,256]{0,1:T(8,128)S(1)}, f32[1024,256]{0,1:T(8,128)S(1)}, u32[]{:S(2)}, u32[]{:S(2)}) %collective-permute-start) | collective-permute-done | bytes 1048608 | tf_op jit(solution)/shard_map/while/body/eval_jaxpr/ppermute | solution.py:59
  301.1 21.9 %while.100 = (s32[]{:T(128)}, f32[2048]{0:T(1024)S(1)}, f32[2048]{0:T(1024)S(1)}, f32[2048,128]{1,0:T(8,128)}, pred[]{:T(512)}, /*index=5*/f32[1024,256]{0,1:T(8...) while((s32[]{:T(128)}, f32[2048]{0:T(1024)S(1)}, ...), condition=%wide.region_15.15_spmd, body=%wide.region_12.14_spmd.sunk | while | flops 1893208064 | bytes 35651772 | solution.py:128
  332.9 5.6 %all-to-all-start.3 = ((f32[1024,2,128]{2,1,0:T(2,128)}), f32[1024,2,128]{2,1,0:T(2,128)}, u32[]{:S(2)}, u32[]{:S(2)}) async-start(f32[1024,2,128]{2,1,0:T(2,128)} %copy.211), calls=%async_computation.3 | async-start | bytes 2097152 | tf_op jit(solution)/shard_map/all_to_all | solution.py:234
  343.4 12.5 %collective-permute-done.3 = f32[4,128,128]{2,1,0:T(8,128)} collective-permute-done((f32[4,128,128]{2,1,0:T(8,128)}, f32[4,128,128]{2,1,0:T(8,128)}, u32[]{:S(2)}, u32[]{:S(2)}) %collective-permute-start.3) | collective-permute-done | bytes 262176 | tf_op jit(solution)/shard_map/ppermute | solution.py:30
  359.6 6.6 %collective-permute-done.4 = f32[4,128,128]{2,1,0:T(8,128)S(1)} collective-permute-done((f32[4,128,128]{2,1,0:T(8,128)}, f32[4,128,128]{2,1,0:T(8,128)S(1)}, u32[]{:S(2)}, u32[]{:S(2)}) %collective-permute-start.4) | collective-permute-done | bytes 262176 | tf_op jit(solution)/shard_map/ppermute | solution.py:30
  371.0 7.2 %collective-permute-done.5 = f32[4,128,128]{2,1,0:T(8,128)S(1)} collective-permute-done((f32[4,128,128]{2,1,0:T(8,128)S(1)}, f32[4,128,128]{2,1,0:T(8,128)S(1)}, u32[]{:S(2)}, u32[]{:S(2)}) %collective-permute-start.5) | collective-permute-done | bytes 262176 | tf_op jit(solution)/shard_map/ppermute | solution.py:30
  389.3 6.7 %collective-permute-done.7 = f32[4,128,128]{2,1,0:T(8,128)S(1)} collective-permute-done((f32[4,128,128]{2,1,0:T(8,128)S(1)}, f32[4,128,128]{2,1,0:T(8,128)S(1)}, u32[]{:S(2)}, u32[]{:S(2)}) %collective-permute-start.7) | collective-permute-done | bytes 262176 | tf_op jit(solution)/shard_map/ppermute | solution.py:30
  397.5 7.9 %all-to-all-start.4 = ((f32[8,128,2]{1,2,0:T(2,128)}), f32[8,128,2]{1,2,0:T(2,128)S(1)}, u32[]{:S(2)}, u32[]{:S(2)}) async-start(f32[8,128,2]{1,2,0:T(2,128)} %bitcast.66), calls=%async_computation.4 | async-start | bytes 16384 | tf_op jit(solution)/shard_map/all_to_all | solution.py:236
  405.4 50.5 %while.95 = (s32[]{:T(128)}, f32[4,512,128]{1,2,0:T(8,128)S(1)}, f32[4,512]{1,0:T(4,128)S(1)}, f32[4,512]{1,0:T(4,128)S(1)}, f32[4,512,128]{2,1,0:T(8,128)S(1)},...) while((s32[]{:T(128)}, f32[4,512,128]{1,2,0:T(8,128)S(1)}, ...), condition=%wide.region_6.7_spmd, body=%wide.region_3.6_spmd.sunk | while | flops 875302912 | bytes 15991019 | solution.py:187
  (349 shorter events, 217.0 us)
Async XLA Ops:
  6.5 44.3 %copy-start.8 = (bf16[128,4,128]{2,1,0:T(4,128)(2,1)S(1)}, bf16[128,4,128]{2,1,0:T(4,128)(2,1)}, u32[]{:S(2)}) copy-start(bf16[128,4,128]{2,1,0:T(4,128)(2,1)} %param.18) | copy-start | bytes 393220
  6.5 44.1 %copy-start.13 = (bf16[128,4,128]{2,1,0:T(4,128)(2,1)S(1)}, bf16[128,4,128]{2,1,0:T(4,128)(2,1)}, u32[]{:S(2)}) copy-start(bf16[128,4,128]{2,1,0:T(4,128)(2,1)} %param.16) | copy-start | bytes 393220
  6.5 96.2 %all-gather.6.cloned.1.call-start = ((), (), s32[]{:S(2)}) async-start(), calls=%async_computation.6 | async-start | bytes 2359296 | tf_op jit(solution)/shard_map/all_gather | solution.py:43
  58.4 57.4 %copy-start.3 = (f32[4,4,128,128]{3,2,1,0:T(8,128)}, f32[4,4,128,128]{3,2,1,0:T(8,128)S(1)}, u32[]{:S(2)}) copy-start(f32[4,4,128,128]{3,2,1,0:T(8,128)S(1)} %convolution_subtract_fusion.1) | copy-start | bytes 3145732
  117.8 29.2 %all-to-all-start.1 = ((f32[128,8,2,128]{3,0,2,1:T(8,128)}), f32[128,8,2,128]{3,0,2,1:T(8,128)S(1)}, u32[]{:S(2)}, u32[]{:S(2)}) async-start(f32[128,8,2,128]{3,0,2,1:T(8,128)} %bitcast.229), calls=%async_computation.1 | async-start | bytes 2097152 | tf_op jit(solution)/shard_map/all_to_all | solution.py:209
  136.5 17.6 %copy-start.5 = (f32[4,128,128]{2,1,0:T(8,128)S(1)}, f32[4,128,128]{2,1,0:T(8,128)}, u32[]{:S(2)}) copy-start(f32[4,128,128]{2,1,0:T(8,128)} %convolution_subtract_fusion.3) | copy-start | bytes 786436
  149.1 55.1 %all-to-all-start = ((f32[128,8,256]{0,2,1:T(8,128)}), f32[128,8,256]{0,2,1:T(8,128)}, u32[]{:S(2)}, u32[]{:S(2)}) async-start(f32[128,8,256]{0,2,1:T(8,128)} %bitcast.228), calls=%async_computation | async-start | bytes 2097152 | tf_op jit(solution)/shard_map/all_to_all | solution.py:210
  154.1 251.4 %all-gather.4.cloned.1.call-start = ((), (), s32[]{:S(2)}) async-start(), calls=%async_computation.5 | async-start | bytes 4718592 | tf_op jit(solution)/shard_map/all_gather | solution.py:167
  154.1 30.3 %collective-permute-start.1 = (f32[4,128,128]{2,1,0:T(8,128)S(1)}, f32[4,128,128]{2,1,0:T(8,128)}, u32[]{:S(2)}, u32[]{:S(2)}) collective-permute-start(f32[4,128,128]{2,1,0:T(8,128)S(1)} %copy-done.5), channel_id=1, source_target_pairs={{0,1},{1,2},{2,3},{3,4},{4,5},{5,6},{6,7},{7,0},{8,9},{9,10},{10,1... | collective-permute-start | bytes 786440 | tf_op jit(solution)/shard_map/ppermute | solution.py:30
  184.3 154.8 %collective-permute-start.2 = (f32[4,128,128]{2,1,0:T(8,128)}, f32[4,128,128]{2,1,0:T(8,128)}, u32[]{:S(2)}, u32[]{:S(2)}) collective-permute-start(f32[4,128,128]{2,1,0:T(8,128)} %collective-permute-done.1), channel_id=1, source_target_pairs={{0,1},{1,2},{2,3},{3,4},{4,5},{5,6},{6,7},{7,0},{8,9},{9,10},{10,1... | collective-permute-start | bytes 786440 | tf_op jit(solution)/shard_map/ppermute | solution.py:30
  207.2 120.7 %copy-start.18 = (f32[4,4,128]{2,1,0:T(4,128)S(1)}, f32[4,4,128]{2,1,0:T(4,128)}, u32[]{:S(2)}) copy-start(f32[4,4,128]{2,1,0:T(4,128)} %get-tuple-element.785) | copy-start | bytes 24580
  207.2 120.7 %copy-start.6 = (f32[4,128,128]{2,1,0:T(8,128)S(1)}, f32[4,128,128]{2,1,0:T(8,128)}, u32[]{:S(2)}) copy-start(f32[4,128,128]{2,1,0:T(8,128)} %convolution_subtract_fusion.3) | copy-start | bytes 786436
  207.2 16.2 %collective-permute-start = (f32[1024,256]{0,1:T(8,128)S(1)}, f32[1024,256]{0,1:T(8,128)S(1)}, u32[]{:S(2)}, u32[]{:S(2)}) collective-permute-start(f32[1024,256]{0,1:T(8,128)S(1)} %get-tuple-element.1099), channel_id=1, source_target_pairs={{0,8},{8,16},{16,24},{1,9},{9,17},{17,25},{2,10},{10,18},{18,26},{... | collective-permute-start | bytes 3145736 | tf_op jit(solution)/shard_map/while/body/eval_jaxpr/ppermute | solution.py:59
  246.2 16.1 %collective-permute-start = (f32[1024,256]{0,1:T(8,128)S(1)}, f32[1024,256]{0,1:T(8,128)S(1)}, u32[]{:S(2)}, u32[]{:S(2)}) collective-permute-start(f32[1024,256]{0,1:T(8,128)S(1)} %get-tuple-element.1099), channel_id=1, source_target_pairs={{0,8},{8,16},{16,24},{1,9},{9,17},{17,25},{2,10},{10,18},{18,26},{... | collective-permute-start | bytes 3145736 | tf_op jit(solution)/shard_map/while/body/eval_jaxpr/ppermute | solution.py:59
  285.0 16.1 %collective-permute-start = (f32[1024,256]{0,1:T(8,128)S(1)}, f32[1024,256]{0,1:T(8,128)S(1)}, u32[]{:S(2)}, u32[]{:S(2)}) collective-permute-start(f32[1024,256]{0,1:T(8,128)S(1)} %get-tuple-element.1099), channel_id=1, source_target_pairs={{0,8},{8,16},{16,24},{1,9},{9,17},{17,25},{2,10},{10,18},{18,26},{... | collective-permute-start | bytes 3145736 | tf_op jit(solution)/shard_map/while/body/eval_jaxpr/ppermute | solution.py:59
  324.4 8.5 %all-to-all-start.2 = ((f32[8,128,2]{1,2,0:T(2,128)}), f32[8,128,2]{1,2,0:T(2,128)S(1)}, u32[]{:S(2)}, u32[]{:S(2)}) async-start(f32[8,128,2]{1,2,0:T(2,128)} %bitcast.54), calls=%async_computation.2 | async-start | bytes 16384 | tf_op jit(solution)/shard_map/all_to_all | solution.py:235
  332.9 64.6 %all-to-all-start.3 = ((f32[1024,2,128]{2,1,0:T(2,128)}), f32[1024,2,128]{2,1,0:T(2,128)}, u32[]{:S(2)}, u32[]{:S(2)}) async-start(f32[1024,2,128]{2,1,0:T(2,128)} %copy.211), calls=%async_computation.3 | async-start | bytes 2097152 | tf_op jit(solution)/shard_map/all_to_all | solution.py:234
  339.1 16.7 %collective-permute-start.3 = (f32[4,128,128]{2,1,0:T(8,128)}, f32[4,128,128]{2,1,0:T(8,128)}, u32[]{:S(2)}, u32[]{:S(2)}) collective-permute-start(f32[4,128,128]{2,1,0:T(8,128)} %collective-permute-done.2), channel_id=1, source_target_pairs={{0,1},{1,2},{2,3},{3,4},{4,5},{5,6},{6,7},{7,0},{8,9},{9,10},{10,1... | collective-permute-start | bytes 786440 | tf_op jit(solution)/shard_map/ppermute | solution.py:30
  343.0 26.5 %copy-start.10 = (bf16[128,4,128]{0,2,1:T(8,128)(2,1)S(1)}, bf16[128,4,128]{0,2,1:T(8,128)(2,1)}, u32[]{:S(2)}) copy-start(bf16[128,4,128]{0,2,1:T(8,128)(2,1)} %copy-done.9) | copy-start | bytes 393220
  355.9 10.4 %collective-permute-start.4 = (f32[4,128,128]{2,1,0:T(8,128)}, f32[4,128,128]{2,1,0:T(8,128)S(1)}, u32[]{:S(2)}, u32[]{:S(2)}) collective-permute-start(f32[4,128,128]{2,1,0:T(8,128)} %collective-permute-done.3), channel_id=1, source_target_pairs={{0,1},{1,2},{2,3},{3,4},{4,5},{5,6},{6,7},{7,0},{8,9},{9,10},{10,1... | collective-permute-start | bytes 786440 | tf_op jit(solution)/shard_map/ppermute | solution.py:30
  366.2 11.9 %collective-permute-start.5 = (f32[4,128,128]{2,1,0:T(8,128)S(1)}, f32[4,128,128]{2,1,0:T(8,128)S(1)}, u32[]{:S(2)}, u32[]{:S(2)}) collective-permute-start(f32[4,128,128]{2,1,0:T(8,128)S(1)} %collective-permute-done.4), channel_id=1, source_target_pairs={{0,1},{1,2},{2,3},{3,4},{4,5},{5,6},{6,7},{7,0},{8,9},{9,10},{10,1... | collective-permute-start | bytes 786440 | tf_op jit(solution)/shard_map/ppermute | solution.py:30
  378.1 8.8 %collective-permute-start.6 = (f32[4,128,128]{2,1,0:T(8,128)S(1)}, f32[4,128,128]{2,1,0:T(8,128)S(1)}, u32[]{:S(2)}, u32[]{:S(2)}) collective-permute-start(f32[4,128,128]{2,1,0:T(8,128)S(1)} %collective-permute-done.5), channel_id=1, source_target_pairs={{0,1},{1,2},{2,3},{3,4},{4,5},{5,6},{6,7},{7,0},{8,9},{9,10},{10,1... | collective-permute-start | bytes 786440 | tf_op jit(solution)/shard_map/ppermute | solution.py:30
  386.9 9.1 %collective-permute-start.7 = (f32[4,128,128]{2,1,0:T(8,128)S(1)}, f32[4,128,128]{2,1,0:T(8,128)S(1)}, u32[]{:S(2)}, u32[]{:S(2)}) collective-permute-start(f32[4,128,128]{2,1,0:T(8,128)S(1)} %collective-permute-done.6), channel_id=1, source_target_pairs={{0,1},{1,2},{2,3},{3,4},{4,5},{5,6},{6,7},{7,0},{8,9},{9,10},{10,1... | collective-permute-start | bytes 786440 | tf_op jit(solution)/shard_map/ppermute | solution.py:30
  397.5 59.9 %all-to-all-start.4 = ((f32[8,128,2]{1,2,0:T(2,128)}), f32[8,128,2]{1,2,0:T(2,128)S(1)}, u32[]{:S(2)}, u32[]{:S(2)}) async-start(f32[8,128,2]{1,2,0:T(2,128)} %bitcast.66), calls=%async_computation.4 | async-start | bytes 16384 | tf_op jit(solution)/shard_map/all_to_all | solution.py:236
  (23 other events, 78.9 us)
Sparse Core Ops, SparseCore 0:
  53.4 49.3 all-gather.5
  157.8 94.5 all-gather.3
